TPU v7x, 32 devices: a whole 2x2x4 slice. The times are simulated.
32 devices in a mesh: seq: 16 (over z, y, core), head: 2 (over x).
Axes of the slice: x: 2, y: 2, z: 4, core: 2. Of those that a mesh axis runs over, the one named last changes fastest.
Arguments:
- tokens: bfloat16 [8192, 5120], P(('seq', 'head')), may hold values from -6 to 6
- w_qkv: bfloat16 [3, 5120, 640], P(None, None, 'head'), may hold values from -0.078125 to 0.078125
- scale_exp: int32 [3, 40, 2], P(None, None, 'head'), may hold values from -2 to 1
- gate_mask: int32 [8192, 2], P('seq', 'head'), may hold values 0 or 1
- rate: float32 [2], P('head'), may hold values from 0.00044194172 to 0.0022097088
- fast_gate: bfloat16 [2, 320, 640], P('head'), may hold values from -0.3125 to 0.3125
- fast_up: bfloat16 [2, 320, 640], P('head'), may hold values from -0.3125 to 0.3125
- fast_down: bfloat16 [2, 320, 640], P('head'), may hold values from -0.25 to 0.25
Outputs:
- answers: bfloat16 [8192, 640], P(('seq', 'head'))
All inputs are finite; a program needn't handle non-finite values. No bound on the sum of `gate_mask` on one device may be relied on, other than what follows from the above.
Results may differ from a plain program's by a relative error of at most 0.012.
Values may be sent and summed in bfloat16 or wider, within the bound.
A program may use at most 64 MiB of HBM per device.

v0:
```python
import jax
import jax.numpy as jnp
from jax import lax
from jax.sharding import PartitionSpec as P


def local_grads(keys, values, weight, old):
    gate = jnp.dot(keys, old[0], preferred_element_type=jnp.float32)
    upper = jnp.dot(keys, old[1], preferred_element_type=jnp.float32)
    sigma = jax.nn.sigmoid(gate)
    active = gate * sigma
    hidden = (active * upper).astype(jnp.bfloat16)
    weighted = (weight[:, None] * values.astype(jnp.float32)).astype(jnp.bfloat16)
    d_hidden = jnp.dot(weighted, old[2], preferred_element_type=jnp.float32)
    d_gate = (d_hidden * upper * sigma * (1.0 + gate * (1.0 - sigma))).astype(jnp.bfloat16)
    d_upper = (d_hidden * active).astype(jnp.bfloat16)
    dims = (((0,), (0,)), ((), ()))
    grad_gate = lax.dot_general(keys, d_gate, dims, preferred_element_type=jnp.float32)
    grad_upper = lax.dot_general(keys, d_upper, dims, preferred_element_type=jnp.float32)
    grad_down = lax.dot_general(weighted, hidden, dims, preferred_element_type=jnp.float32)
    return jnp.stack([grad_gate, grad_upper, grad_down])


def respond(query, renorm):
    gate = jnp.dot(query, renorm[0], preferred_element_type=jnp.float32)
    upper = jnp.dot(query, renorm[1], preferred_element_type=jnp.float32)
    hidden = (jax.nn.silu(gate) * upper).astype(jnp.bfloat16)
    output = lax.dot_general(
        hidden, renorm[2], (((1,), (1,)), ((), ())), preferred_element_type=jnp.float32
    )
    scaled = output * lax.rsqrt(jnp.mean(output * output, axis=-1, keepdims=True) + 1e-05)
    return scaled.astype(jnp.bfloat16)


def body(tokens, w_qkv, scale_exp, gate_mask, rate, fast_gate, fast_up, fast_down):
    factor = jnp.exp2(scale_exp.astype(jnp.float32))[:, :, 0]
    block_rows = w_qkv.shape[1] // factor.shape[1]
    factor = jnp.repeat(factor, block_rows, axis=1)[:, :, None].astype(jnp.bfloat16)
    weff = w_qkv * factor
    triple = jnp.einsum(
        "rd,cdh->rch",
        lax.all_gather(tokens, "head", axis=0, tiled=True),
        weff,
        preferred_element_type=jnp.float32,
    ).astype(jnp.bfloat16)
    query = triple[:, 0]
    keys = triple[:, 1]
    values = triple[:, 2]
    weight = rate[0] * gate_mask[:, 0].astype(jnp.float32)
    old = jnp.stack([fast_gate[0], fast_up[0], fast_down[0]])
    partial_grads = local_grads(keys, values, weight, old)
    old_f = old.astype(jnp.float32)
    old_norm = jnp.sqrt(jnp.sum(old_f * old_f, axis=1))
    total = lax.psum(partial_grads, "seq")
    fresh = old_f + total
    new_sq = jnp.sum(fresh * fresh, axis=1)
    renorm = (fresh * (old_norm / jnp.sqrt(new_sq + 1e-06))[:, None, :]).astype(jnp.bfloat16)
    answer = respond(query, renorm)
    return lax.all_to_all(answer, "head", split_axis=0, concat_axis=1, tiled=True)


def solution(mesh):
    in_specs = (
        P(("seq", "head"), None),
        P(None, None, "head"),
        P(None, None, "head"),
        P("seq", "head"),
        P("head"),
        P("head", None, None),
        P("head", None, None),
        P("head", None, None),
    )
    out_specs = P(("seq", "head"), None)
    return jax.shard_map(body, mesh=mesh, in_specs=in_specs, out_specs=out_specs, check_vma=False)
```

profile of v0, /device:TPU:1, one launch (start us, length us, event | category | flops | bytes accessed | tf_op | source)
XLA Modules:
  0.0 215.5 jit_solution(169645211959964053)
XLA Ops:
  6.5 0.0 copy-start.5
  6.5 0.0 copy-start.4
  6.5 0.0 all-gather.2.cloned.1.call-start
  6.5 0.7 all-gather.2.cloned.1.call-update
  7.3 0.0 all-reduce.2.cloned.1.call-start
  8.0 0.0 copy-done.5
  8.0 0.1 broadcast_bitcast_fusion
  8.1 0.0 copy-done.4
  8.1 71.2 %all-gather.2.cloned.1.call-done = bf16[512,5120]{1,0:T(8,128)(2,1)} async-done(((bf16[256,5120]{1,0:T(8,128)(2,1)}), bf16[512,5120]{1,0:T(8,128)(2,1)}) %all-gather.2.cloned.1.call-update) | async-done | bytes 5242896 | tf_op jit(solution)/shard_map/all_gather | solution.py:42
  79.3 0.0 copy-start.2
  79.3 9.5 %fusion.10 = bf16[512,3,320]{0,2,1:T(8,128)(2,1)S(1)} fusion(bf16[512,5120]{1,0:T(8,128)(2,1)} %all-gather.2.cloned.1.call-done, bf16[3,5120,320]{1,2,0:T(8,128)(2,1)} %param.9, bf16[3,5120]{1,0:T(4,128)(2,1)S(1)} %bitcast.82), kind=kOutput, calls=%fused_computation.12 | convolution fusion | flops 5038571520 | bytes 16087040 | tf_op jit(solution)/shard_map/rd,cdh->rch/dot_general | solution.py:40
  88.9 0.0 copy-done.2
  88.9 0.0 copy-start.1
  88.9 0.6 fusion.23
  89.5 0.4 copy-done.1
  89.9 0.0 copy-start.3
  89.9 0.6 fusion.25
  90.5 0.4 copy-done.3
  90.9 0.6 fusion.27
  91.5 0.6 convolution_bitcast_fusion.1
  92.1 0.8 convolution_bitcast_fusion.2
  92.9 0.6 convolution_bitcast_fusion
  93.5 1.6 pad_maximum_fusion
  95.1 0.0 all-reduce.2.cloned.1.call-update
  95.1 98.9 %all-reduce.2.cloned.1.call-done = f32[3,320,640]{2,1,0:T(8,128)} async-done(((f32[3,320,640]{2,1,0:T(8,128)}), f32[3,320,640]{2,1,0:T(8,128)}) %all-reduce.2.cloned.1.call-update) | async-done | bytes 2457616 | tf_op jit(solution)/shard_map/psum | solution.py:54
  194.0 0.0 copy-start
  194.0 2.4 %fusion.4 = (f32[3,640]{1,0:T(4,128)S(1)}, f32[3,640]{1,0:T(4,128)S(1)}) fusion(bf16[1,320,640]{2,1,0:T(8,128)(2,1)S(1)} %copy-done.3, bf16[1,320,640]{2,1,0:T(8,128)(2,1)S(1)} %copy-done.1, bf16[1,320,640]{2,1,0:T(8,128)(2,1)S(1)} %copy-done.2, f32[3,320,640]{2,1,0:T(8,128)} %all-reduce.2.cloned.1.call-done), kind=kLoop, calls=%fused_computation.6 | loop fusion | flops 4911360 | bytes 3701760 | tf_op jit(solution)/shard_map/reduce_sum | solution.py:53
  196.4 0.1 copy-done
  196.5 0.4 multiply_convert_fusion
  196.8 1.6 fusion.22
  198.5 2.3 %multiply_reduce_fusion.1 = (f32[512]{0:T(512)S(1)}, f32[512,320]{0,1:T(8,128)S(1)}) fusion(bf16[3,320,640]{2,1,0:T(8,128)(2,1)S(1)} %multiply_convert_fusion, f32[512,640]{1,0:T(8,128)} %fusion.22, bf16[512,3,320]{0,2,1:T(8,128)(2,1)S(1)} %fusion.10), kind=kOutput, calls=%fused_computation.30 | convolution fusion | flops 421723648 | bytes 3115008 | tf_op jit(solution)/shard_map/dot_general | solution.py:28
  200.8 0.1 multiply_convert_fusion.6
  200.9 6.8 %all_to_all.19 = bf16[2,256,320]{1,2,0:T(8,128)(2,1)S(1)} all-to-all(bf16[2,256,320]{1,2,0:T(8,128)(2,1)S(1)} %bitcast.79), channel_id=1, replica_groups=mesh['seq'=16,'head'=2] {'head'}, dimensions={0} | all-to-all | bytes 655360 | tf_op jit(solution)/shard_map/all_to_all | solution.py:59
  207.7 0.9 copy.11
  (7 shorter events, 0.1 us)
Async XLA Ops:
  6.5 1.4 copy-start.5
  6.5 1.6 copy-start.4
  6.5 72.8 %all-gather.2.cloned.1.call-start = ((), (), s32[]{:S(2)}) async-start(), calls=%async_computation.1 | async-start | bytes 7864320 | tf_op jit(solution)/shard_map/all_gather | solution.py:42
  7.3 186.8 %all-reduce.2.cloned.1.call-start = ((), (), s32[]{:S(2)}) async-start(), calls=%async_computation.2 | async-start | bytes 4915200 | tf_op jit(solution)/shard_map/psum | solution.py:54
  79.3 9.5 %copy-start.2 = (bf16[1,320,640]{2,1,0:T(8,128)(2,1)S(1)}, bf16[1,320,640]{2,1,0:T(8,128)(2,1)}, u32[]{:S(2)}) copy-start(bf16[1,320,640]{2,1,0:T(8,128)(2,1)} %param.13) | copy-start | bytes 1228804
  88.9 1.0 copy-start.1
  89.9 1.0 copy-start.3
  194.0 2.4 %copy-start = (f32[3,320,640]{2,1,0:T(8,128)S(1)}, f32[3,320,640]{2,1,0:T(8,128)}, u32[]{:S(2)}) copy-start(f32[3,320,640]{2,1,0:T(8,128)} %all-reduce.2.cloned.1.call-done) | copy-start | bytes 7372804
Sparse Core Ops, SparseCore 0:
  8.9 70.4 all-gather.1
  95.3 98.7 all-reduce.1
where the time goes:
time: 219 us; the launch traced here: 215 us
  waiting for transfers between devices  171 us (78%)
  matrix products  17.3 us (8%)
  between operations  14.2 us (6%)
  blocking collectives  6.77 us (3%)
  other arithmetic  4.41 us (2%)
    psum x1, waiting for transfers between devices, body(): total = lax.psum(partial_grads, 'seq')  98.9 us
    all_gather x1, waiting for transfers between devices, body(): lax.all_gather(tokens, 'head', axis=0, tiled=True)  71.2 us
    dot_general x1, matrix products, body(): jnp.einsum('rd,cdh->rch', lax.all_gather(tokens, 'head', axis=0, tiled=Tr...  9.52 us
    all_to_all x1, blocking collectives, body(): lax.all_to_all(answer, 'head', split_axis=0, concat_axis=1, tiled=True)  6.77 us
  transfers between devices with their start and end apart: 2, of which 2 were waited for; matrix products, arithmetic and copies ran while one was open for 0% of the time, Pallas kernels for 0%

commit v1 on v0

v1 whole, which is shorter than its diff:
```python
import functools

import jax
import jax.numpy as jnp
from jax import lax
from jax.experimental import pallas as pl
from jax.experimental.pallas import tpu as pltpu
from jax.sharding import PartitionSpec as P

MESH = pl.DeviceIdType.MESH
F32 = jnp.float32
BF16 = jnp.bfloat16


def dot(a, b, lhs=1, rhs=0):
    return lax.dot_general(a, b, (((lhs,), (rhs,)), ((), ())), preferred_element_type=F32)


def plan(seq, rows):
    factors = (2, seq // 8, 4)
    padded = -(-rows // (16 * seq)) * 16 * seq
    chunks = max(1, min(2, padded // (16 * seq)))
    while (padded // chunks) % (16 * seq):
        chunks -= 1
    return factors, padded, chunks


def kernel(
    sizes,
    tokens_ref, w_hbm, exp_ref, mask_ref, rate_ref, g_ref, u_ref, d_ref,
    out_ref,
    toks, w, acc, grads, buf, tot, recv_c, recv_y, recv_z, renorm, a_send, a_recv,
    tok_sem, w_sem, tsend, trecv, rs_send, rs_recv, ag_send, ag_recv, asend, arecv,
):
    heads, seq, kc, nk, sb, factors, padded, chunks = sizes
    t, hd = tokens_ref.shape[0], w_hbm.shape[2]
    s, me = lax.axis_index("seq"), lax.axis_index("head")
    strides = (1, factors[0], factors[0] * factors[1])
    digits = tuple(lax.rem(lax.div(s, st), f) for st, f in zip(strides, factors))

    def member(phase, step):
        f, st = factors[phase], strides[phase]
        digit = lax.rem(digits[phase] + step, f)
        return digit, (s + (digit - digits[phase]) * st, me)

    def head_peer(step):
        return (s, lax.rem(me + step, heads))

    def tok_copy(k):
        cols = pl.ds(pl.multiple_of(k * kc, kc), kc)
        return pltpu.make_async_copy(tokens_ref.at[:, cols], toks.at[0, :, cols], tok_sem.at[k])

    def w_copy(k):
        rows = pl.ds(pl.multiple_of(k * kc, kc), kc)
        return pltpu.make_async_copy(w_hbm.at[:, rows, :], w.at[:, rows, :], w_sem.at[k])

    def tok_send(step, k):
        cols = pl.ds(pl.multiple_of(k * kc, kc), kc)
        return pltpu.make_async_remote_copy(
            src_ref=tokens_ref.at[:, cols],
            dst_ref=toks.at[heads - step, :, cols],
            send_sem=tsend.at[step - 1, k],
            recv_sem=trecv.at[heads - step - 1, k],
            device_id=head_peer(step),
            device_id_type=MESH,
        )

    def tok_arrival(slot, k):
        cols = pl.ds(pl.multiple_of(k * kc, kc), kc)
        return pltpu.make_async_remote_copy(
            src_ref=tokens_ref.at[:, cols],
            dst_ref=toks.at[slot, :, cols],
            send_sem=tsend.at[slot - 1, k],
            recv_sem=trecv.at[slot - 1, k],
            device_id=head_peer(slot),
            device_id_type=MESH,
        )

    barrier = pltpu.get_barrier_semaphore()
    partners = [head_peer(step) for step in range(1, heads)]
    for phase in range(3):
        partners += [member(phase, step)[1] for step in range(1, factors[phase])]
    for partner in partners:
        pl.semaphore_signal(barrier, inc=1, device_id=partner, device_id_type=MESH)

    def load(k, carry):
        tok_copy(k).start()
        w_copy(k).start()
        return carry

    lax.fori_loop(0, nk, load, 0)
    pl.semaphore_wait(barrier, len(partners))

    def send(k, carry):
        for step in range(1, heads):
            tok_send(step, k).start()
        return carry

    lax.fori_loop(0, nk, send, 0)

    acc[...] = jnp.zeros_like(acc)

    def project(slot, k):
        cols = pl.ds(pl.multiple_of(k * kc, kc), kc)
        x = toks[slot, :, cols]
        for c in range(3):
            acc[c, slot] += dot(x, w[c, cols, :])

    def own(k, carry):
        tok_copy(k).wait()
        w_copy(k).wait()
        for b in range(kc // sb):
            rows = pl.ds(pl.multiple_of(k * kc + b * sb, sb), sb)
            for c in range(3):
                e = exp_ref[c, k * (kc // sb) + b]
                factor = jnp.exp2(jnp.full((1, hd), e, jnp.int32).astype(F32)).astype(BF16)
                w[c, rows, :] = (w[c, rows, :].astype(F32) * factor.astype(F32)).astype(BF16)
        project(0, k)
        return carry

    lax.fori_loop(0, nk, own, 0)
    rate = rate_ref[0]

    def add_grads(slot):
        owner = lax.rem(me + slot, heads)
        mask = mask_ref[pl.ds(pl.multiple_of(owner * t, t), t), :]
        keys = acc[1, slot].astype(BF16)
        values = acc[2, slot].astype(BF16)
        gate = dot(keys, g_ref[0])
        upper = dot(keys, u_ref[0])
        sigma = jax.nn.sigmoid(gate)
        active = gate * sigma
        hidden = (active * upper).astype(BF16)
        weighted = ((rate * mask.astype(F32)) * values.astype(F32)).astype(BF16)
        d_hidden = dot(weighted, d_ref[0])
        d_gate = (d_hidden * upper * sigma * (1.0 + gate * (1.0 - sigma))).astype(BF16)
        d_upper = (d_hidden * active).astype(BF16)
        grads[0] += dot(keys, d_gate, 0, 0)
        grads[1] += dot(keys, d_upper, 0, 0)
        grads[2] += dot(weighted, hidden, 0, 0)

    grads[...] = jnp.zeros_like(grads)
    add_grads(0)

    def others(k, carry):
        for slot in range(1, heads):
            tok_arrival(slot, k).wait_recv()
            project(slot, k)
        return carry

    lax.fori_loop(0, nk, others, 0)

    def other_grads(slot, carry):
        add_grads(slot)
        return carry

    lax.fori_loop(1, heads, other_grads, 0)

    n = hd
    for m in range(3):
        buf[m * n : (m + 1) * n, :] = grads[m].astype(BF16)
    if padded > 3 * n:
        buf[3 * n :, :] = jnp.zeros((padded - 3 * n, buf.shape[1]), BF16)
    span = padded // chunks
    recvs = (recv_c, recv_y, recv_z)

    def region(chunk, phase):
        off, size = chunk * span, span
        for p in range(phase):
            size //= factors[p]
            off = off + digits[p] * size
        return off, size

    def rs_copies(chunk, phase):
        off, size = region(chunk, phase)
        part = size // factors[phase]
        copies = []
        for step in range(1, factors[phase]):
            digit, device = member(phase, step)
            slot = factors[phase] - step - 1
            copies.append(pltpu.make_async_remote_copy(
                src_ref=buf.at[pl.ds(pl.multiple_of(off + digit * part, 16), part), :],
                dst_ref=recvs[phase].at[chunk, slot],
                send_sem=rs_send.at[chunk, phase, step - 1],
                recv_sem=rs_recv.at[chunk, phase, slot],
                device_id=device,
                device_id_type=MESH,
            ))
        return copies

    def rs_finish(chunk, phase, copies):
        for copy in copies:
            copy.wait_recv()
        off, size = region(chunk, phase + 1)
        mine = pl.ds(pl.multiple_of(off, 16), size)
        total = buf[mine, :].astype(F32)
        for slot in range(factors[phase] - 1):
            total = total + recvs[phase][chunk, slot].astype(F32)
        target = tot if phase == 2 else buf
        target[mine, :] = total.astype(BF16)

    def ag_copies(chunk, phase):
        off, size = region(chunk, phase + 1)
        mine = pl.ds(pl.multiple_of(off, 16), size)
        copies = []
        for step in range(1, factors[phase]):
            _, device = member(phase, step)
            copies.append(pltpu.make_async_remote_copy(
                src_ref=tot.at[mine, :],
                dst_ref=tot.at[mine, :],
                send_sem=ag_send.at[chunk, phase, step - 1],
                recv_sem=ag_recv.at[chunk, phase, factors[phase] - step - 1],
                device_id=device,
                device_id_type=MESH,
            ))
        return copies

    def start(copies):
        for copy in copies:
            copy.start()
        return copies

    every = []
    flight = {}
    for tick in range(6 + chunks - 1):
        for chunk in range(chunks):
            stage = tick - chunk
            if stage < 0 or stage > 6:
                continue
            if 1 <= stage <= 3:
                rs_finish(chunk, stage - 1, flight[chunk])
            elif stage > 3:
                for copy in flight[chunk]:
                    copy.wait_recv()
            if stage < 3:
                flight[chunk] = start(rs_copies(chunk, stage))
            elif stage < 6:
                flight[chunk] = start(ag_copies(chunk, 5 - stage))
            every += flight[chunk] if stage < 6 else []
    for chunk in range(chunks):
        stage = 6 + chunks - 1 - chunk
        if stage == 6:
            for copy in flight[chunk]:
                copy.wait_recv()

    for m, ref in enumerate((g_ref, u_ref, d_ref)):
        old = ref[0].astype(F32)
        fresh = old + tot[m * n : (m + 1) * n, :].astype(F32)
        old_norm = jnp.sqrt(jnp.sum(old * old, axis=0, keepdims=True))
        new_norm = jnp.sqrt(jnp.sum(fresh * fresh, axis=0, keepdims=True) + 1e-6)
        renorm[m] = (fresh * (old_norm / new_norm)).astype(BF16)

    def respond(slot):
        query = acc[0, slot].astype(BF16)
        gate = dot(query, renorm[0])
        upper = dot(query, renorm[1])
        hidden = (gate * jax.nn.sigmoid(gate) * upper).astype(BF16)
        output = dot(hidden, renorm[2], 1, 1)
        return (output * lax.rsqrt(jnp.mean(output * output, axis=-1, keepdims=True) + 1e-5)).astype(BF16)

    answers = []
    for step in range(1, heads):
        a_send[step - 1] = respond(step)
        copy = pltpu.make_async_remote_copy(
            src_ref=a_send.at[step - 1],
            dst_ref=a_recv.at[heads - step],
            send_sem=asend.at[step - 1],
            recv_sem=arecv.at[heads - step - 1],
            device_id=head_peer(step),
            device_id_type=MESH,
        )
        copy.start()
        answers.append(copy)
    a_recv[0] = respond(0)
    for copy in answers:
        copy.wait_recv()
    for h in range(heads):
        slot = lax.rem(h - me + heads, heads)
        out_ref[:, h * hd : (h + 1) * hd] = a_recv[slot]

    for copy in answers + every:
        copy.wait_send()

    def sent(k, carry):
        for step in range(1, heads):
            tok_send(step, k).wait_send()
        return carry

    lax.fori_loop(0, nk, sent, 0)


def body(mesh, tokens, w_qkv, scale_exp, gate_mask, rate, fast_gate, fast_up, fast_down):
    heads, seq = mesh.shape["head"], mesh.shape["seq"]
    t, d = tokens.shape
    hd, hid = fast_gate.shape[1:]
    blocks = scale_exp.shape[1]
    sb = d // blocks
    kc = sb * (4 if blocks % 4 == 0 else 1)
    nk = d // kc
    factors, padded, chunks = plan(seq, 3 * hd)
    span = padded // chunks
    parts = []
    size = span
    for f in factors:
        size //= f
        parts.append(size)
    dma = pltpu.SemaphoreType.DMA
    vmem = pl.BlockSpec(memory_space=pltpu.VMEM)
    smem = pl.BlockSpec(memory_space=pltpu.SMEM)
    hbm = pl.BlockSpec(memory_space=pl.ANY)
    most = max(factors) - 1
    return pl.pallas_call(
        functools.partial(kernel, (heads, seq, kc, nk, sb, factors, padded, chunks)),
        out_shape=jax.ShapeDtypeStruct((t, heads * hd), BF16),
        in_specs=[hbm, hbm, smem, vmem, smem, vmem, vmem, vmem],
        out_specs=vmem,
        scratch_shapes=[
            pltpu.VMEM((heads, t, d), BF16),
            pltpu.VMEM((3, d, hd), BF16),
            pltpu.VMEM((3, heads, t, hd), F32),
            pltpu.VMEM((3, hd, hid), F32),
            pltpu.VMEM((padded, hid), BF16),
            pltpu.VMEM((padded, hid), BF16),
            pltpu.VMEM((chunks, factors[0] - 1, parts[0], hid), BF16),
            pltpu.VMEM((chunks, factors[1] - 1, parts[1], hid), BF16),
            pltpu.VMEM((chunks, factors[2] - 1, parts[2], hid), BF16),
            pltpu.VMEM((3, hd, hid), BF16),
            pltpu.VMEM((heads - 1, t, hd), BF16),
            pltpu.VMEM((heads, t, hd), BF16),
            dma((nk,)),
            dma((nk,)),
            dma((heads - 1, nk)),
            dma((heads - 1, nk)),
            dma((chunks, 3, most)),
            dma((chunks, 3, most)),
            dma((chunks, 3, most)),
            dma((chunks, 3, most)),
            dma((heads - 1,)),
            dma((heads - 1,)),
        ],
        compiler_params=pltpu.CompilerParams(
            collective_id=0, has_side_effects=True, vmem_limit_bytes=60 * 1024 * 1024
        ),
    )(
        tokens, w_qkv, scale_exp.reshape(scale_exp.shape[:2]), gate_mask, rate,
        fast_gate, fast_up, fast_down,
    )


def solution(mesh):
    in_specs = (
        P(("seq", "head"), None),
        P(None, None, "head"),
        P(None, None, "head"),
        P("seq", "head"),
        P("head"),
        P("head", None, None),
        P("head", None, None),
        P("head", None, None),
    )
    out_specs = P(("seq", "head"), None)
    return jax.shard_map(
        functools.partial(body, mesh), mesh=mesh, in_specs=in_specs, out_specs=out_specs, check_vma=False
    )
```

time: 219 us -> 124 us (0.57); the launches traced: 215 us -> 124 us
  waiting for transfers between devices: 171 us -> 0 us
  Pallas kernels: 0 us -> 104 us
  matrix products: 17.3 us -> 0 us
  local copies, waits for them, and re-layouts: 1.91 us -> 18.9 us
  between operations: 14.2 us -> 0.66 us
  blocking collectives: 6.77 us -> 0 us
  other arithmetic: 4.41 us -> 0 us
    pallas_call x0 -> x1, Pallas kernels: none -> 104 us  [body(): pl.pallas_call(functools.partial(kernel, (heads, seq, kc, nk, sb, factors...]
    psum x1 -> x0, waiting for transfers between devices: 98.9 us -> none  [body(): total = lax.psum(partial_grads, 'seq')]
    all_gather x1 -> x0, waiting for transfers between devices: 71.2 us -> none  [body(): lax.all_gather(tokens, 'head', axis=0, tiled=True)]
    unnamed x15 -> x4, local copies, waits for them, and re-layouts: 0.99 us -> 18.9 us
    dot_general x9 -> x0, matrix products: 17.3 us -> none  [the longest x1 9.52 us: body(): jnp.einsum('rd,cdh->rch', lax.all_gather(tokens, 'head', axis=0, tiled=Tr...]
    all_to_all x1 -> x0, blocking collectives: 6.77 us -> none  [body(): lax.all_to_all(answer, 'head', split_axis=0, concat_axis=1, tiled=True)]
    reduce_sum x1 -> x0, other arithmetic: 2.35 us -> none  [body(): old_norm = jnp.sqrt(jnp.sum(old_f * old_f, axis=1))]
  transfers between devices with their start and end apart: 2 -> 0, of which waited for: 2 -> 0; matrix products, arithmetic and copies ran while one was open for 0% -> 0% of each run, Pallas kernels for 0% -> 0%
where the time goes in v1:
time: 124 us
  Pallas kernels  104 us (84%)
  local copies, waits for them, and re-layouts  18.9 us (15%)
    pallas_call x1, Pallas kernels, body(): pl.pallas_call(functools.partial(kernel, (heads, seq, kc, nk, sb, factors...  104 us
    unnamed x4, local copies, waits for them, and re-layouts  18.9 us

profile of v1, /device:TPU:1, one launch (start us, length us, event | category | flops | bytes accessed | tf_op | source)
XLA Modules:
  0.0 123.6 jit_solution(17848724595307462555)
XLA Ops:
  0.7 1.2 copy.13
  1.9 1.5 %copy.10.mask_ref = s32[512,1]{1,0:T(8,128)} copy(s32[512,1]{0,1:T(1,128)} %param.11) | data formatting | bytes 4096 | tf_op args[3]
  3.4 14.4 %copy.9.w_hbm = bf16[3,5120,320]{2,1,0:T(8,128)(2,1)} copy(bf16[3,5120,320]{1,2,0:T(8,128)(2,1)} %param.9) | data formatting | bytes 19660800 | tf_op args[1]
  17.8 104.0 %shard_map.82 = bf16[256,640]{1,0:T(8,128)(2,1)} custom-call(bf16[256,5120]{1,0:T(8,128)(2,1)} %tokens_ref.1, bf16[3,5120,320]{2,1,0:T(8,128)(2,1)} %copy.9.w_hbm, s32[3,40]{1,0:T(4,128)} %bitcast.3, s32[512,1]{1,0:T(8,128)} %copy.10.mask_ref, f32[1]{0:T(128)S(6)} %copy.15.rate_ref, bf16[1,320,640]{2,1,0:T(8,128)(2,1)} %g_ref.1, bf16[1,320,640]{2,1,0:T(8,128)(2,1)} %u_ref.1, ...), custom_call_target="tpu_custom_call" | custom-call | tf_op jit(solution)/shard_map/pallas_call | solution.py:312
  121.8 1.7 %copy.16 = bf16[256,640]{1,0:T(8,128)(2,1)} copy(bf16[256,640]{1,0:T(8,128)(2,1)} %shard_map.82) | data formatting | bytes 655360

commit v2 on v1

--- a/solution.py
+++ b/solution.py
@@ -29,11 +29,11 @@
     sizes,
     tokens_ref, w_hbm, exp_ref, mask_ref, rate_ref, g_ref, u_ref, d_ref,
     out_ref,
-    toks, w, acc, grads, buf, tot, recv_c, recv_y, recv_z, renorm, a_send, a_recv,
+    toks, w, acc, grads, buf, tot, recv_c, recv_y, recv_z, renorm, a_send, a_recv, weights,
     tok_sem, w_sem, tsend, trecv, rs_send, rs_recv, ag_send, ag_recv, asend, arecv,
 ):
     heads, seq, kc, nk, sb, factors, padded, chunks = sizes
-    t, hd = tokens_ref.shape[0], w_hbm.shape[2]
+    t, hd = tokens_ref.shape[0], w_hbm.shape[1]
     s, me = lax.axis_index("seq"), lax.axis_index("head")
     strides = (1, factors[0], factors[0] * factors[1])
     digits = tuple(lax.rem(lax.div(s, st), f) for st, f in zip(strides, factors))
@@ -51,8 +51,8 @@
         return pltpu.make_async_copy(tokens_ref.at[:, cols], toks.at[0, :, cols], tok_sem.at[k])
 
     def w_copy(k):
-        rows = pl.ds(pl.multiple_of(k * kc, kc), kc)
-        return pltpu.make_async_copy(w_hbm.at[:, rows, :], w.at[:, rows, :], w_sem.at[k])
+        cols = pl.ds(pl.multiple_of(k * kc, kc), kc)
+        return pltpu.make_async_copy(w_hbm.at[:, :, cols], w.at[:, :, cols], w_sem.at[k])
 
     def tok_send(step, k):
         cols = pl.ds(pl.multiple_of(k * kc, kc), kc)
@@ -104,26 +104,28 @@
         cols = pl.ds(pl.multiple_of(k * kc, kc), kc)
         x = toks[slot, :, cols]
         for c in range(3):
-            acc[c, slot] += dot(x, w[c, cols, :])
+            acc[c, slot] += dot(x, w[c, :, cols], 1, 1)
 
     def own(k, carry):
         tok_copy(k).wait()
         w_copy(k).wait()
         for b in range(kc // sb):
-            rows = pl.ds(pl.multiple_of(k * kc + b * sb, sb), sb)
+            cols = pl.ds(pl.multiple_of(k * kc + b * sb, sb), sb)
             for c in range(3):
-                e = exp_ref[c, k * (kc // sb) + b]
-                factor = jnp.exp2(jnp.full((1, hd), e, jnp.int32).astype(F32)).astype(BF16)
-                w[c, rows, :] = (w[c, rows, :].astype(F32) * factor.astype(F32)).astype(BF16)
+                e = exp_ref[c, 0, k * (kc // sb) + b]
+                factor = jnp.exp2(jnp.full((1, sb), e, jnp.int32).astype(F32)).astype(BF16)
+                w[c, :, cols] = (w[c, :, cols].astype(F32) * factor.astype(F32)).astype(BF16)
         project(0, k)
         return carry
 
     lax.fori_loop(0, nk, own, 0)
-    rate = rate_ref[0]
+    weights[...] = jnp.transpose(
+        jnp.broadcast_to(rate_ref[0] * mask_ref[...].astype(F32), (128, heads * t))
+    )
 
     def add_grads(slot):
         owner = lax.rem(me + slot, heads)
-        mask = mask_ref[pl.ds(pl.multiple_of(owner * t, t), t), :]
+        weight = weights[pl.ds(pl.multiple_of(owner * t, t), t), :1]
         keys = acc[1, slot].astype(BF16)
         values = acc[2, slot].astype(BF16)
         gate = dot(keys, g_ref[0])
@@ -131,7 +133,7 @@
         sigma = jax.nn.sigmoid(gate)
         active = gate * sigma
         hidden = (active * upper).astype(BF16)
-        weighted = ((rate * mask.astype(F32)) * values.astype(F32)).astype(BF16)
+        weighted = (weight * values.astype(F32)).astype(BF16)
         d_hidden = dot(weighted, d_ref[0])
         d_gate = (d_hidden * upper * sigma * (1.0 + gate * (1.0 - sigma))).astype(BF16)
         d_upper = (d_hidden * active).astype(BF16)
@@ -316,7 +318,7 @@
         out_specs=vmem,
         scratch_shapes=[
             pltpu.VMEM((heads, t, d), BF16),
-            pltpu.VMEM((3, d, hd), BF16),
+            pltpu.VMEM((3, hd, d), BF16),
             pltpu.VMEM((3, heads, t, hd), F32),
             pltpu.VMEM((3, hd, hid), F32),
             pltpu.VMEM((padded, hid), BF16),
@@ -327,6 +329,7 @@
             pltpu.VMEM((3, hd, hid), BF16),
             pltpu.VMEM((heads - 1, t, hd), BF16),
             pltpu.VMEM((heads, t, hd), BF16),
+            pltpu.VMEM((heads * t, 128), F32),
             dma((nk,)),
             dma((nk,)),
             dma((heads - 1, nk)),
@@ -342,7 +345,7 @@
             collective_id=0, has_side_effects=True, vmem_limit_bytes=60 * 1024 * 1024
         ),
     )(
-        tokens, w_qkv, scale_exp.reshape(scale_exp.shape[:2]), gate_mask, rate,
+        tokens, w_qkv.swapaxes(1, 2), scale_exp.swapaxes(1, 2), gate_mask.swapaxes(0, 1), rate,
         fast_gate, fast_up, fast_down,
     )
 

time: 124 us -> 107 us (0.86)
  local copies, waits for them, and re-layouts: 18.9 us -> 1.73 us
    unnamed x4 -> x1, local copies, waits for them, and re-layouts: 18.9 us -> 1.73 us
where the time goes in v2:
time: 107 us; the launch traced here: 106 us
  Pallas kernels  104 us (97%)
  local copies, waits for them, and re-layouts  1.73 us (2%)
    pallas_call x1, Pallas kernels, body(): pl.pallas_call(functools.partial(kernel, (heads, seq, kc, nk, sb, factors...  104 us

profile of v2, /device:TPU:1, one launch (start us, length us, event | category | flops | bytes accessed | tf_op | source)
XLA Modules:
  0.0 106.3 jit_solution(7990738872261747908)
XLA Ops:
  0.7 103.9 %shard_map.82 = bf16[256,640]{1,0:T(8,128)(2,1)} custom-call(bf16[256,5120]{1,0:T(8,128)(2,1)} %tokens_ref.1, bf16[3,320,5120]{2,1,0:T(8,128)(2,1)} %bitcast.3, s32[3,1,40]{2,1,0:T(1,128)} %bitcast.5, s32[1,512]{1,0:T(1,128)} %bitcast.4, f32[1]{0:T(128)S(6)} %copy.10.rate_ref, bf16[1,320,640]{2,1,0:T(8,128)(2,1)} %g_ref.1, bf16[1,320,640]{2,1,0:T(8,128)(2,1)} %u_ref.1, ...), custom_call_target="tpu_custom_call" | custom-call | tf_op jit(solution)/shard_map/pallas_call | solution.py:314
  104.6 1.7 %copy.11 = bf16[256,640]{1,0:T(8,128)(2,1)} copy(bf16[256,640]{1,0:T(8,128)(2,1)} %shard_map.82) | data formatting | bytes 655360

commit v3 on v2

--- a/solution.py
+++ b/solution.py
@@ -25,14 +25,24 @@
     return factors, padded, chunks
 
 
+def shared_depth(heads, seq, d, hd, kc):
+    unit = 128 * (seq // 2)
+    if heads != 2 or hd % 32 or unit % kc:
+        return 0
+    return (4 * d // 10) // unit * unit
+
+
 def kernel(
     sizes,
     tokens_ref, w_hbm, exp_ref, mask_ref, rate_ref, g_ref, u_ref, d_ref,
     out_ref,
     toks, w, acc, grads, buf, tot, recv_c, recv_y, recv_z, renorm, a_send, a_recv, weights,
+    wsl, wx, pacc, p_send, p_recv,
     tok_sem, w_sem, tsend, trecv, rs_send, rs_recv, ag_send, ag_recv, asend, arecv,
+    l_sem, xs, xr, zs, zr, ys, yr, cs, cr, ps, pr,
 ):
-    heads, seq, kc, nk, sb, factors, padded, chunks = sizes
+    heads, seq, kc, nk, sb, factors, padded, chunks, depth = sizes
+    first = depth // kc
     t, hd = tokens_ref.shape[0], w_hbm.shape[1]
     s, me = lax.axis_index("seq"), lax.axis_index("head")
     strides = (1, factors[0], factors[0] * factors[1])
@@ -88,15 +98,134 @@
         w_copy(k).start()
         return carry
 
+    every = []
+
+    def start(copies):
+        for copy in copies:
+            copy.start()
+        every.extend(copies)
+        return copies
+
+    core, y, z = digits
+    half, width = hd // 2, wsl.shape[2]
+    chip = y + factors[1] * z
+
+    def piece(m, zrel, yrel, c):
+        at = lax.rem(y + yrel, factors[1]) + factors[1] * lax.rem(z + zrel, factors[2])
+        return wx.at[
+            m,
+            pl.ds(pl.multiple_of(c * half, 16), half),
+            pl.ds(pl.multiple_of(at * width, 128), width),
+        ]
+
+    def remote(src, dst, send_sem, recv_sem, device):
+        return pltpu.make_async_remote_copy(
+            src_ref=src, dst_ref=dst, send_sem=send_sem, recv_sem=recv_sem,
+            device_id=device, device_id_type=MESH,
+        )
+
+    def over_x(m):
+        return remote(wsl.at[m], piece(m, 0, 0, core), xs.at[m], xr.at[m], head_peer(1))
+
+    def along_z(m, step):
+        own_piece = piece(m, 0, 0, core)
+        return remote(own_piece, own_piece, zs.at[m, step - 1], zr.at[m, factors[2] - step - 1], member(2, step)[1])
+
+    def z_arrival(m, slot):
+        where = piece(m, slot + 1, 0, core)
+        return remote(where, where, zs.at[m, slot], zr.at[m, slot], member(2, 1)[1])
+
+    def over_y(m, zrel, step):
+        where = piece(m, zrel, 0, core)
+        return remote(where, where, ys.at[m, zrel, step - 1], yr.at[m, zrel, factors[1] - step - 1], member(1, step)[1])
+
+    def y_arrival(m, zrel, slot):
+        where = piece(m, zrel, slot + 1, core)
+        return remote(where, where, ys.at[m, zrel, slot], yr.at[m, zrel, slot], member(1, 1)[1])
+
+    def to_core(m, zrel, yrel):
+        where = piece(m, zrel, yrel, core)
+        return remote(where, where, cs.at[m, zrel, yrel], cr.at[m, zrel, yrel], member(0, 1)[1])
+
+    def core_arrival(m, zrel, yrel):
+        where = piece(m, zrel, yrel, 1 - core)
+        return remote(where, where, cs.at[m, zrel, yrel], cr.at[m, zrel, yrel], member(0, 1)[1])
+
+    def forward(m, zrel):
+        start([over_y(m, zrel, step) for step in range(1, factors[1])] + [to_core(m, zrel, 0)])
+
+    def take_x(m):
+        over_x(m).wait_recv()
+        start([along_z(m, step) for step in range(1, factors[2])])
+        forward(m, 0)
+
+    def take_z(m):
+        for slot in range(factors[2] - 1):
+            z_arrival(m, slot).wait_recv()
+            forward(m, slot + 1)
+
+    def take_y(m):
+        for zrel in range(factors[2]):
+            for slot in range(factors[1] - 1):
+                y_arrival(m, zrel, slot).wait_recv()
+                start([to_core(m, zrel, slot + 1)])
+
+    def partial_copy(m):
+        return remote(p_send.at[m], p_recv.at[m], ps.at[m], pr.at[m], head_peer(1))
+
+    def answer_partial(m):
+        for zrel in range(factors[2]):
+            for yrel in range(factors[1]):
+                core_arrival(m, zrel, yrel).wait_recv()
+        pacc[...] = jnp.zeros_like(pacc)
+
+        def add(k, carry):
+            cols = pl.ds(pl.multiple_of(k * kc, kc), kc)
+            pacc[...] += dot(toks[0, :, cols], wx[m, :, cols], 1, 1)
+            return carry
+
+        lax.fori_loop(0, first, add, 0)
+        p_send[m] = pacc[...].astype(BF16)
+        start([partial_copy(m)])
+
+    def take_partial(m):
+        partial_copy(m).wait_recv()
+        acc[m, 1] += p_recv[m].astype(F32)
+
+    def factor_of(c, block):
+        e = jnp.full((1, sb), exp_ref[c, 0, block], jnp.int32).astype(F32)
+        return jnp.exp2(e).astype(BF16).astype(F32)
+
+    if depth:
+        w_slice = pltpu.make_async_copy(
+            w_hbm.at[
+                :,
+                pl.ds(pl.multiple_of(core * half, 16), half),
+                pl.ds(pl.multiple_of(chip * width, 128), width),
+            ],
+            wsl, l_sem.at[0],
+        )
+        w_slice.start()
     lax.fori_loop(0, nk, load, 0)
+    if depth:
+        w_slice.wait()
+        for c in range(3):
+            for b in range(width // sb):
+                cols = pl.ds(b * sb, sb)
+                scale = factor_of(c, chip * (width // sb) + b)
+                wsl[c, :, cols] = (wsl[c, :, cols].astype(F32) * scale).astype(BF16)
     pl.semaphore_wait(barrier, len(partners))
+    if depth:
+        start([over_x(m) for m in (1, 2, 0)])
+        for m in (1, 2, 0):
+            take_x(m)
 
     def send(k, carry):
         for step in range(1, heads):
             tok_send(step, k).start()
         return carry
 
-    lax.fori_loop(0, nk, send, 0)
+    lax.fori_loop(first, nk, send, 0)
 
     acc[...] = jnp.zeros_like(acc)
 
@@ -112,9 +241,8 @@
         for b in range(kc // sb):
             cols = pl.ds(pl.multiple_of(k * kc + b * sb, sb), sb)
             for c in range(3):
-                e = exp_ref[c, 0, k * (kc // sb) + b]
-                factor = jnp.exp2(jnp.full((1, sb), e, jnp.int32).astype(F32)).astype(BF16)
-                w[c, :, cols] = (w[c, :, cols].astype(F32) * factor.astype(F32)).astype(BF16)
+                scale = factor_of(c, k * (kc // sb) + b)
+                w[c, :, cols] = (w[c, :, cols].astype(F32) * scale).astype(BF16)
         project(0, k)
         return carry
 
@@ -144,13 +272,25 @@
     grads[...] = jnp.zeros_like(grads)
     add_grads(0)
 
+    if depth:
+        take_z(1)
+        take_z(2)
+        take_y(1)
+        answer_partial(1)
+        take_y(2)
+        answer_partial(2)
+        take_z(0)
+
     def others(k, carry):
         for slot in range(1, heads):
             tok_arrival(slot, k).wait_recv()
             project(slot, k)
         return carry
 
-    lax.fori_loop(0, nk, others, 0)
+    lax.fori_loop(first, nk, others, 0)
+    if depth:
+        take_partial(1)
+        take_partial(2)
 
     def other_grads(slot, carry):
         add_grads(slot)
@@ -217,12 +357,6 @@
             ))
         return copies
 
-    def start(copies):
-        for copy in copies:
-            copy.start()
-        return copies
-
-    every = []
     flight = {}
     for tick in range(6 + chunks - 1):
         for chunk in range(chunks):
@@ -238,7 +372,9 @@
                 flight[chunk] = start(rs_copies(chunk, stage))
             elif stage < 6:
                 flight[chunk] = start(ag_copies(chunk, 5 - stage))
-            every += flight[chunk] if stage < 6 else []
+        if depth and tick == 2:
+            take_y(0)
+            answer_partial(0)
     for chunk in range(chunks):
         stage = 6 + chunks - 1 - chunk
         if stage == 6:
@@ -260,6 +396,8 @@
         output = dot(hidden, renorm[2], 1, 1)
         return (output * lax.rsqrt(jnp.mean(output * output, axis=-1, keepdims=True) + 1e-5)).astype(BF16)
 
+    if depth:
+        take_partial(0)
     answers = []
     for step in range(1, heads):
         a_send[step - 1] = respond(step)
@@ -288,7 +426,7 @@
             tok_send(step, k).wait_send()
         return carry
 
-    lax.fori_loop(0, nk, sent, 0)
+    lax.fori_loop(first, nk, sent, 0)
 
 
 def body(mesh, tokens, w_qkv, scale_exp, gate_mask, rate, fast_gate, fast_up, fast_down):
@@ -311,8 +449,11 @@
     smem = pl.BlockSpec(memory_space=pltpu.SMEM)
     hbm = pl.BlockSpec(memory_space=pl.ANY)
     most = max(factors) - 1
+    depth = shared_depth(heads, seq, d, hd, kc)
+    width = max(depth // (seq // 2), 128)
+    f1, f2 = factors[1:]
     return pl.pallas_call(
-        functools.partial(kernel, (heads, seq, kc, nk, sb, factors, padded, chunks)),
+        functools.partial(kernel, (heads, seq, kc, nk, sb, factors, padded, chunks, depth)),
         out_shape=jax.ShapeDtypeStruct((t, heads * hd), BF16),
         in_specs=[hbm, hbm, smem, vmem, smem, vmem, vmem, vmem],
         out_specs=vmem,
@@ -330,6 +471,11 @@
             pltpu.VMEM((heads - 1, t, hd), BF16),
             pltpu.VMEM((heads, t, hd), BF16),
             pltpu.VMEM((heads * t, 128), F32),
+            pltpu.VMEM((3, hd // 2, width), BF16),
+            pltpu.VMEM((3, hd, max(depth, 128)), BF16),
+            pltpu.VMEM((t, hd), F32),
+            pltpu.VMEM((3, t, hd), BF16),
+            pltpu.VMEM((3, t, hd), BF16),
             dma((nk,)),
             dma((nk,)),
             dma((heads - 1, nk)),
@@ -340,6 +486,17 @@
             dma((chunks, 3, most)),
             dma((heads - 1,)),
             dma((heads - 1,)),
+            dma((1,)),
+            dma((3,)),
+            dma((3,)),
+            dma((3, f2 - 1)),
+            dma((3, f2 - 1)),
+            dma((3, f2, f1 - 1)),
+            dma((3, f2, f1 - 1)),
+            dma((3, f2, f1)),
+            dma((3, f2, f1)),
+            dma((3,)),
+            dma((3,)),
         ],
         compiler_params=pltpu.CompilerParams(
             collective_id=0, has_side_effects=True, vmem_limit_bytes=60 * 1024 * 1024

time: 107 us -> 99.4 us (0.929)
  Pallas kernels: 104 us -> 96.9 us
    pallas_call x1, Pallas kernels: 104 us -> 96.9 us  [body(): pl.pallas_call(functools.partial(kernel, (heads, seq, kc, nk, sb, factors...]
where the time goes in v3:
time: 99.4 us; the launch traced here: 99.3 us
  Pallas kernels  96.9 us (97%)
  local copies, waits for them, and re-layouts  1.73 us (2%)
    pallas_call x1, Pallas kernels, body(): pl.pallas_call(functools.partial(kernel, (heads, seq, kc, nk, sb, factors...  96.9 us

profile of v3, /device:TPU:1, one launch (start us, length us, event | category | flops | bytes accessed | tf_op | source)
XLA Modules:
  0.0 99.3 jit_solution(7596128848862288249)
XLA Ops:
  0.7 96.9 %shard_map.82 = bf16[256,640]{1,0:T(8,128)(2,1)} custom-call(bf16[256,5120]{1,0:T(8,128)(2,1)} %tokens_ref.1, bf16[3,320,5120]{2,1,0:T(8,128)(2,1)} %bitcast.3, s32[3,1,40]{2,1,0:T(1,128)} %bitcast.5, s32[1,512]{1,0:T(1,128)} %bitcast.4, f32[1]{0:T(128)S(6)} %copy.10.rate_ref, bf16[1,320,640]{2,1,0:T(8,128)(2,1)} %g_ref.1, bf16[1,320,640]{2,1,0:T(8,128)(2,1)} %u_ref.1, ...), custom_call_target="tpu_custom_call" | custom-call | tf_op jit(solution)/shard_map/pallas_call | solution.py:455
  97.5 1.7 %copy.11 = bf16[256,640]{1,0:T(8,128)(2,1)} copy(bf16[256,640]{1,0:T(8,128)(2,1)} %shard_map.82) | data formatting | bytes 655360

commit v4 on v3

--- a/solution.py
+++ b/solution.py
@@ -29,7 +29,7 @@
     unit = 128 * (seq // 2)
     if heads != 2 or hd % 32 or unit % kc:
         return 0
-    return (4 * d // 10) // unit * unit
+    return (6 * d // 10) // unit * unit
 
 
 def kernel(
@@ -247,6 +247,8 @@
         return carry
 
     lax.fori_loop(0, nk, own, 0)
+    if depth:
+        take_z(1)
     weights[...] = jnp.transpose(
         jnp.broadcast_to(rate_ref[0] * mask_ref[...].astype(F32), (128, heads * t))
     )
@@ -269,12 +271,12 @@
         grads[1] += dot(keys, d_upper, 0, 0)
         grads[2] += dot(weighted, hidden, 0, 0)
 
+    if depth:
+        take_z(2)
     grads[...] = jnp.zeros_like(grads)
     add_grads(0)
 
     if depth:
-        take_z(1)
-        take_z(2)
         take_y(1)
         answer_partial(1)
         take_y(2)
@@ -372,7 +374,7 @@
                 flight[chunk] = start(rs_copies(chunk, stage))
             elif stage < 6:
                 flight[chunk] = start(ag_copies(chunk, 5 - stage))
-        if depth and tick == 2:
+        if depth and tick == 4:
             take_y(0)
             answer_partial(0)
     for chunk in range(chunks):

time: 99.4 us -> 98.4 us (0.990)
  Pallas kernels: 96.9 us -> 95.9 us
    pallas_call x1, Pallas kernels: 96.9 us -> 95.9 us  [body(): pl.pallas_call(functools.partial(kernel, (heads, seq, kc, nk, sb, factors...]
where the time goes in v4:
time: 98.4 us; the launch traced here: 98.3 us
  Pallas kernels  95.9 us (97%)
  local copies, waits for them, and re-layouts  1.73 us (2%)
    pallas_call x1, Pallas kernels, body(): pl.pallas_call(functools.partial(kernel, (heads, seq, kc, nk, sb, factors...  95.9 us

profile of v4, /device:TPU:1, one launch (start us, length us, event | category | flops | bytes accessed | tf_op | source)
XLA Modules:
  0.0 98.3 jit_solution(539849842259106798)
XLA Ops:
  0.7 95.9 %shard_map.82 = bf16[256,640]{1,0:T(8,128)(2,1)} custom-call(bf16[256,5120]{1,0:T(8,128)(2,1)} %tokens_ref.1, bf16[3,320,5120]{2,1,0:T(8,128)(2,1)} %bitcast.3, s32[3,1,40]{2,1,0:T(1,128)} %bitcast.5, s32[1,512]{1,0:T(1,128)} %bitcast.4, f32[1]{0:T(128)S(6)} %copy.10.rate_ref, bf16[1,320,640]{2,1,0:T(8,128)(2,1)} %g_ref.1, bf16[1,320,640]{2,1,0:T(8,128)(2,1)} %u_ref.1, ...), custom_call_target="tpu_custom_call" | custom-call | tf_op jit(solution)/shard_map/pallas_call | solution.py:457
  96.5 1.7 %copy.11 = bf16[256,640]{1,0:T(8,128)(2,1)} copy(bf16[256,640]{1,0:T(8,128)(2,1)} %shard_map.82) | data formatting | bytes 655360
